TPU v7x, 32 devices: a whole 2x2x4 slice. The times are simulated.
32 devices in a mesh: grp: 4 (over y, core), seq: 8 (over z, x).
Axes of the slice: x: 2, y: 2, z: 4, core: 2. Of those that a mesh axis runs over, the one named last changes fastest.
Arguments:
- queries: bfloat16 [16384, 512], P(('grp', 'seq')), may hold values from -8 to 8
- keys: bfloat16 [16384, 512], P(('grp', 'seq')), may hold values from -4.5 to 4.5
- values: bfloat16 [16384, 512], P(('grp', 'seq')), may hold values from -6 to 6
- resid: bfloat16 [16384, 1024], P(('grp', 'seq')), may hold values from -54 to 54
- w_out: bfloat16 [512, 1024], replicated, may hold values from -2 to 2
- block_lang: int32 [256], P(('grp', 'seq')), may hold values from 0 to 11, as said below
- w_down: bfloat16 [12, 1024, 384], P('grp', 'seq'), may hold values from -0.1875 to 0.1875
- w_up: bfloat16 [12, 384, 1024], P('grp', None, 'seq'), may hold values from -0.3125 to 0.3125
- bias_down: bfloat16 [12, 384], P('grp'), may hold values from -4 to 4
- cotangent: bfloat16 [16384, 1024], P(('grp', 'seq')), may hold values from -6 to 6
Outputs:
- grad_down: float32 [1024, 12, 384], P('seq', 'grp')
Inputs may be any that keep to these rules, and one draw needn't show every extreme that they name: Block b holds tokens b * 64 to (b + 1) * 64 - 1, and its language's owner group is block_lang[b] // 3. Of the 8 blocks of one device (blocks d * 8 to (d + 1) * 8 - 1), at most 2 have the same owner group; for every index along seq, some owner group has a block from the device of that index in every group.
All inputs are finite; a program needn't handle non-finite values.
Results may differ from a plain program's by a relative error of at most 0.022.
Values may be sent and summed in bfloat16 or wider, within the bound.
No kernel may reach another device: no remote copies, remote signals or barrier semaphores. Data moves between devices by JAX's collectives and lax.ppermute only.
A program may use at most 128 MiB of HBM per device.

v0:
```python
import math
import jax
import jax.numpy as jnp
from jax import lax
from jax.sharding import PartitionSpec as P

HD = 64
WINDOW = 256
EPSILON = 1e-05


def shifted(value, axis, by):
    size = lax.axis_size(axis)
    pairs = [(i, i + by) for i in range(size) if 0 <= i + by < size]
    return lax.ppermute(value, axis, pairs)


def gelu_slope(pre_act):
    return jax.vjp(jax.nn.gelu, pre_act)[1](jnp.ones_like(pre_act))[0]


def normalize(block_rows):
    widened = block_rows.astype(jnp.float32)
    center = widened - jnp.mean(widened, axis=-1, keepdims=True)
    spread = jnp.mean(center * center, axis=-1, keepdims=True)
    return (center * lax.rsqrt(spread + EPSILON)).astype(jnp.bfloat16)


def body(queries, keys, values, resid, w_out, block_lang, w_down, w_up, bias_down, cotangent):
    tok_dev, width_q = queries.shape
    head_dim = HD
    head_count = width_q // head_dim
    window_len = WINDOW
    k_rim, v_rim = shifted((keys[tok_dev - window_len :], values[tok_dev - window_len :]), "seq", 1)
    key_span = window_len + tok_dev
    q_heads = queries.reshape(tok_dev, head_count, head_dim)
    k_heads = jnp.concatenate([k_rim, keys], axis=0).reshape(key_span, head_count, head_dim)
    v_heads = jnp.concatenate([v_rim, values], axis=0).reshape(key_span, head_count, head_dim)
    scores = jnp.einsum(
        "qhd,khd->hqk", q_heads, k_heads, preferred_element_type=jnp.float32
    ) * head_dim ** (-0.5)
    q_pos = jnp.arange(tok_dev)[:, None] + window_len
    k_pos = jnp.arange(key_span)[None, :]
    first_dev = lax.axis_index("seq") == 0
    allowed = (
        (k_pos <= q_pos)
        & (k_pos > q_pos - window_len)
        & ((k_pos >= window_len) | jnp.logical_not(first_dev))
    )
    scores = jnp.where(allowed[None], scores, -1e30)
    row_max = jnp.max(scores, axis=-1, keepdims=True)
    weights = jnp.exp(scores - row_max) * allowed[None]
    softmax_w = (weights / jnp.sum(weights, axis=-1, keepdims=True)).astype(jnp.bfloat16)
    context = jnp.einsum("hqk,khd->qhd", softmax_w, v_heads, preferred_element_type=jnp.float32)
    context = context.astype(jnp.bfloat16).reshape(tok_dev, width_q)
    hidden = (
        resid.astype(jnp.float32) + jnp.dot(context, w_out, preferred_element_type=jnp.float32)
    ).astype(jnp.bfloat16)
    block_count = block_lang.shape[0]
    block_len = tok_dev // block_count
    group_count = lax.axis_size("grp")
    cap_each = max(1, block_count // group_count)
    slot_count = group_count * cap_each
    lang_grp = w_down.shape[0]
    model_width = hidden.shape[1]
    hidden_units = w_down.shape[2]
    owner_group = block_lang // lang_grp
    block_ids = jnp.arange(block_count)
    earlier = (owner_group[None, :] == owner_group[:, None]) & (
        block_ids[None, :] < block_ids[:, None]
    )
    rank_within = jnp.sum(earlier.astype(jnp.int32), axis=1)
    slot_of = owner_group * cap_each + rank_within
    select_int = (slot_of[None, :] == jnp.arange(slot_count)[:, None]).astype(jnp.int32)
    choose_mat = select_int.astype(jnp.bfloat16)
    outgoing = normalize(hidden)

    def to_slots(token_rows):
        shaped = token_rows.reshape(block_count, block_len, model_width)
        return jnp.einsum(
            "ob,btd->otd", choose_mat, shaped, preferred_element_type=jnp.float32
        ).astype(jnp.bfloat16)

    row_slots = to_slots(outgoing)
    cot_slots = to_slots(cotangent)
    lang_slots = jnp.sum(select_int * block_lang[None, :], axis=1) + jnp.sum(select_int, axis=1) - 1
    got_rows, got_cot, got_lang = (
        lax.all_to_all(row_slots, "grp", split_axis=0, concat_axis=0, tiled=True),
        lax.all_to_all(cot_slots, "grp", split_axis=0, concat_axis=0, tiled=True),
        lax.all_to_all(lang_slots, "grp", split_axis=0, concat_axis=0, tiled=True),
    )
    down_all, up_all = (
        lax.all_gather(w_down, "seq", axis=1, tiled=True),
        lax.all_gather(w_up, "seq", axis=2, tiled=True),
    )
    live_slot = got_lang >= 0
    safe_lang = jnp.where(live_slot, got_lang - lax.axis_index("grp") * lang_grp, 0).astype(
        jnp.int32
    )

    def slot_terms(slot_item):
        slot_rows, slot_cot, language, is_live = slot_item
        down_one = lax.dynamic_index_in_dim(down_all, language, 0, keepdims=False)
        up_one = lax.dynamic_index_in_dim(up_all, language, 0, keepdims=False)
        bias_one = lax.dynamic_index_in_dim(bias_down, language, 0, keepdims=False).astype(
            jnp.float32
        )
        pre_act = jnp.dot(slot_rows, down_one, preferred_element_type=jnp.float32) + bias_one
        back_proj = lax.dot_general(
            slot_cot, up_one, (((1,), (1,)), ((), ())), preferred_element_type=jnp.float32
        )
        gate_grad = (gelu_slope(pre_act) * back_proj * is_live.astype(jnp.float32)).astype(
            jnp.bfloat16
        )
        return (slot_rows, gate_grad)

    normed_all, grad_all = lax.map(slot_terms, (got_rows, got_cot, safe_lang, live_slot))
    inv_scale = 1.0 / math.sqrt(tok_dev * lax.axis_size("seq"))

    def add_slot(slot_idx, running):
        columns = normed_all[slot_idx]
        product = lax.dot_general(
            columns,
            grad_all[slot_idx],
            (((0,), (0,)), ((), ())),
            preferred_element_type=jnp.float32,
        )
        language = safe_lang[slot_idx]
        current = lax.dynamic_index_in_dim(running, language, 1, keepdims=True)
        return lax.dynamic_update_index_in_dim(running, current + product[:, None, :], language, 1)

    start_acc = jnp.zeros(
        (model_width // lax.axis_size("seq") * lax.axis_size("seq"), lang_grp, hidden_units),
        jnp.float32,
    )
    return lax.psum_scatter(
        (lax.fori_loop(0, slot_count, add_slot, start_acc) * inv_scale).astype(jnp.bfloat16),
        "seq",
        scatter_dimension=0,
        tiled=True,
    ).astype(jnp.float32)


def solution(mesh):
    in_specs = (
        P(("grp", "seq"), None),
        P(("grp", "seq"), None),
        P(("grp", "seq"), None),
        P(("grp", "seq"), None),
        P(),
        P(("grp", "seq")),
        P("grp", "seq", None),
        P("grp", None, "seq"),
        P("grp", None),
        P(("grp", "seq"), None),
    )
    out_specs = P("seq", "grp", None)
    return jax.shard_map(body, mesh=mesh, in_specs=in_specs, out_specs=out_specs, check_vma=False)
```

profile of v0, /device:TPU:0, one launch (start us, length us, event | category | flops | bytes accessed | tf_op | source)
XLA Modules:
  0.0 305.9 jit_solution(14016514012558106310)
XLA Ops:
  8.2 5.6 %collective-permute-start.1 = (bf16[256,512]{1,0:T(8,128)(2,1)S(1)}, bf16[256,512]{1,0:T(8,128)(2,1)}, u32[]{:S(2)}, u32[]{:S(2)}) collective-permute-start(bf16[256,512]{1,0:T(8,128)(2,1)S(1)} %slice.7), channel_id=1, source_target_pairs={{0,1},{1,2},{2,3},{3,4},{4,5},{5,6},{6,7},{8,9},{9,10},{10,11},{11... | collective-permute-start | bytes 786440 | tf_op jit(solution)/shard_map/ppermute | solution.py:15
  13.8 1.7 slice.6
  15.5 3.5 %collective-permute-start = (bf16[256,512]{1,0:T(8,128)(2,1)}, bf16[256,512]{1,0:T(8,128)(2,1)}, u32[]{:S(2)}, u32[]{:S(2)}) collective-permute-start(bf16[256,512]{1,0:T(8,128)(2,1)} %slice.6), channel_id=1, source_target_pairs={{0,1},{1,2},{2,3},{3,4},{4,5},{5,6},{6,7},{8,9},{9,10},{10,11},{11... | collective-permute-start | bytes 786440 | tf_op jit(solution)/shard_map/ppermute | solution.py:15
  22.0 3.2 %all-to-all-start = ((s32[4,2,1]{1,2,0:T(1,128)}), s32[4,2,1]{1,2,0:T(1,128)S(1)}, u32[]{:S(2)}, u32[]{:S(2)}) async-start(s32[4,2,1]{1,2,0:T(1,128)} %bitcast.11), calls=%async_computation | async-start | bytes 4096 | tf_op jit(solution)/shard_map/all_to_all | solution.py:90
  25.9 2.1 copy.50
  28.7 1.6 copy.55
  33.6 11.0 %fusion.53 = (f32[8,512]{1,0:T(8,128)S(1)}, f32[8,512,768]{1,2,0:T(8,128)}) fusion(f32[512,768]{0,1:T(8,128)S(1)} %get-tuple-element.273, bf16[768,8,64]{0,2,1:T(8,128)(2,1)} %bitcast.84, bf16[512,8,64]{0,2,1:T(8,128)(2,1)} %bitcast.86, pred[512,768]{0,1:T(8,128)(4,1)} %get-tuple-element.272), kind=kOutput, calls=%fused_computation.85 | convolution fusion | flops 418382592 | bytes 15876096 | tf_op jit(solution)/shard_map/sub | solution.py:52
  45.9 6.0 %fusion.40 = bf16[8,64,512]{2,1,0:T(8,128)(2,1)S(1)} fusion(bf16[768,8,64]{0,2,1:T(8,128)(2,1)S(1)} %bitcast.85, f32[8,512,768]{1,2,0:T(8,128)} %get-tuple-element.275, f32[8,512]{1,0:T(8,128)S(1)} %get-tuple-element.274), kind=kOutput, calls=%fused_computation.56 | convolution fusion | flops 409206784 | bytes 13910016 | tf_op jit(solution)/shard_map/hqk,khd->qhd/dot_general | solution.py:54
  52.8 3.7 %all-to-all-start.2 = ((bf16[8,64,1024]{2,1,0:T(8,128)(2,1)}), bf16[8,64,1024]{2,1,0:T(8,128)(2,1)S(1)}, u32[]{:S(2)}, u32[]{:S(2)}) async-start(bf16[8,64,1024]{2,1,0:T(8,128)(2,1)} %copy.55), calls=%async_computation.2 | async-start | bytes 2097152 | tf_op jit(solution)/shard_map/all_to_all | solution.py:89
  58.0 1.6 copy.53
  59.5 11.3 %all-to-all-done.2 = bf16[8,64,1024]{2,1,0:T(8,128)(2,1)S(1)} async-done(((bf16[8,64,1024]{2,1,0:T(8,128)(2,1)}), bf16[8,64,1024]{2,1,0:T(8,128)(2,1)S(1)}, u32[]{:S(2)}, u32[]{:S(2)}) %all-to-all-start.2) | async-done | bytes 1048608 | tf_op jit(solution)/shard_map/all_to_all | solution.py:89
  70.8 3.5 %all-to-all-start.1 = ((bf16[8,64,1024]{2,1,0:T(8,128)(2,1)}), bf16[8,64,1024]{2,1,0:T(8,128)(2,1)S(1)}, u32[]{:S(2)}, u32[]{:S(2)}) async-start(bf16[8,64,1024]{2,1,0:T(8,128)(2,1)} %copy.53), calls=%async_computation.1 | async-start | bytes 2097152 | tf_op jit(solution)/shard_map/all_to_all | solution.py:88
  75.9 12.8 %all-to-all-done.1 = bf16[8,64,1024]{2,1,0:T(8,128)(2,1)S(1)} async-done(((bf16[8,64,1024]{2,1,0:T(8,128)(2,1)}), bf16[8,64,1024]{2,1,0:T(8,128)(2,1)S(1)}, u32[]{:S(2)}, u32[]{:S(2)}) %all-to-all-start.1) | async-done | bytes 1048608 | tf_op jit(solution)/shard_map/all_to_all | solution.py:88
  88.7 31.4 %all-gather.5.cloned.1.call-done = bf16[3,384,1024]{2,1,0:T(8,128)(2,1)} async-done(((bf16[3,384,128]{2,1,0:T(8,128)(2,1)}), bf16[3,384,1024]{2,1,0:T(8,128)(2,1)}) %all-gather.5.cloned.1.call-update) | async-done | bytes 2359312 | tf_op jit(solution)/shard_map/all_gather | solution.py:94
  120.1 61.8 %while.25 = (s32[]{:T(128)}, bf16[8,64,384]{2,1,0:T(8,128)(2,1)S(1)}, bf16[8,64,1024]{2,1,0:T(8,128)(2,1)S(1)}, s32[8]{0:T(128)S(1)}, bf16[3,1024,384]{2,1,0:T(8...) while((s32[]{:T(128)}, ...), condition=%wide.region_8.9_spmd, body=%wide.region_7.8_spmd.sunk | while | flops 101179776 | bytes 2087354 | solution.py:117
  122.9 1.4 convolution_add_fusion.2
  124.2 1.3 dynamic_slice.120
  126.3 1.5 fusion.73
  130.6 1.4 convolution_add_fusion.2
  132.0 1.3 dynamic_slice.120
  134.0 1.5 fusion.73
  138.3 1.4 convolution_add_fusion.2
  139.7 1.3 dynamic_slice.120
  141.7 1.5 fusion.73
  146.0 1.4 convolution_add_fusion.2
  147.4 1.3 dynamic_slice.120
  149.5 1.5 fusion.73
  153.8 1.4 convolution_add_fusion.2
  157.2 1.5 fusion.73
  161.5 1.4 convolution_add_fusion.2
  164.9 1.5 fusion.73
  169.2 1.4 convolution_add_fusion.2
  172.6 1.5 fusion.73
  176.9 1.4 convolution_add_fusion.2
  180.4 1.5 fusion.73
  181.9 2.4 broadcast_in_dim.50
  184.3 41.2 %while.26 = (s32[]{:T(128)}, f32[1024,3,384]{2,0,1:T(8,128)}, s32[8]{0:T(128)S(1)}, bf16[8,64,1024]{2,1,0:T(8,128)(2,1)S(1)}, bf16[8,64,384]{2,1,0:T(8,128)(2,1)S(1)}, /*index=5*/s32[]{:T(128)}, s32[]{:T(128)}, s32[]{:T(128)}) while((s32[]{:T(128)}, f32[1024,3,384]{2,0,1:T(8,128)}, s32[8]{0:T(128)S(1)}, bf16[8,64,1024]{2,1,0:T(8,128)(2,1)S(1)}, ...), condition=%wide.region_10.11_spmd, body=%wide.region_9.10_spmd.sunk | while | flops 50724868 | bytes 3327111 | solution.py:137
  186.5 3.0 fusion.76
  191.7 3.0 fusion.76
  196.8 2.9 fusion.76
  202.0 2.9 fusion.76
  207.1 2.9 fusion.76
  212.3 2.9 fusion.76
  217.4 3.0 fusion.76
  222.6 2.9 fusion.76
  225.5 4.2 %multiply_convert_fusion = bf16[1024,3,384]{2,0,1:T(8,128)(2,1)} fusion(f32[1024,3,384]{2,0,1:T(8,128)} %get-tuple-element.213), kind=kLoop, calls=%fused_computation.42 | loop fusion | flops 2359296 | bytes 7077888 | tf_op jit(solution)/shard_map/convert_element_type | solution.py:137
  229.7 67.9 %reduce-scatter.2.cloned.1.call-done = bf16[128,3,384]{2,0,1:T(8,128)(2,1)} async-done(((bf16[1024,3,384]{2,0,1:T(8,128)(2,1)}), bf16[128,3,384]{2,0,1:T(8,128)(2,1)}) %reduce-scatter.2.cloned.1.call-update) | async-done | bytes 294928 | tf_op jit(solution)/shard_map/reduce_scatter | solution.py:136
  297.6 1.8 convert_element_type.84
  (77 shorter events, 29.9 us)
Async XLA Ops:
  6.5 21.5 %copy-start = (bf16[512,1024]{1,0:T(8,128)(2,1)S(1)}, bf16[512,1024]{1,0:T(8,128)(2,1)}, u32[]{:S(2)}) copy-start(bf16[512,1024]{1,0:T(8,128)(2,1)} %param.23) | copy-start | bytes 3145732
  6.5 82.2 %all-gather.3.cloned.1.call-start = ((), (), s32[]{:S(2)}) async-start(), calls=%async_computation.4 | async-start | bytes 2654208 | tf_op jit(solution)/shard_map/all_gather | solution.py:93
  8.2 23.2 %collective-permute-start.1 = (bf16[256,512]{1,0:T(8,128)(2,1)S(1)}, bf16[256,512]{1,0:T(8,128)(2,1)}, u32[]{:S(2)}, u32[]{:S(2)}) collective-permute-start(bf16[256,512]{1,0:T(8,128)(2,1)S(1)} %slice.7), channel_id=1, source_target_pairs={{0,1},{1,2},{2,3},{3,4},{4,5},{5,6},{6,7},{8,9},{9,10},{10,11},{11... | collective-permute-start | bytes 786440 | tf_op jit(solution)/shard_map/ppermute | solution.py:15
  15.5 29.1 %collective-permute-start = (bf16[256,512]{1,0:T(8,128)(2,1)}, bf16[256,512]{1,0:T(8,128)(2,1)}, u32[]{:S(2)}, u32[]{:S(2)}) collective-permute-start(bf16[256,512]{1,0:T(8,128)(2,1)} %slice.6), channel_id=1, source_target_pairs={{0,1},{1,2},{2,3},{3,4},{4,5},{5,6},{6,7},{8,9},{9,10},{10,11},{11... | collective-permute-start | bytes 786440 | tf_op jit(solution)/shard_map/ppermute | solution.py:15
  22.0 30.8 %all-to-all-start = ((s32[4,2,1]{1,2,0:T(1,128)}), s32[4,2,1]{1,2,0:T(1,128)S(1)}, u32[]{:S(2)}, u32[]{:S(2)}) async-start(s32[4,2,1]{1,2,0:T(1,128)} %bitcast.11), calls=%async_computation | async-start | bytes 4096 | tf_op jit(solution)/shard_map/all_to_all | solution.py:90
  25.2 94.9 %all-gather.5.cloned.1.call-start = ((), (), s32[]{:S(2)}) async-start(), calls=%async_computation.5 | async-start | bytes 2654208 | tf_op jit(solution)/shard_map/all_gather | solution.py:94
  28.7 2.7 copy-start.1
  33.6 11.0 %copy-start.2 = (bf16[512,512]{1,0:T(8,128)(2,1)S(1)}, bf16[512,512]{1,0:T(8,128)(2,1)}, u32[]{:S(2)}) copy-start(bf16[512,512]{1,0:T(8,128)(2,1)} %param.16) | copy-start | bytes 1572868
  45.9 6.0 %copy-start.4 = (bf16[512,1024]{1,0:T(8,128)(2,1)S(1)}, bf16[512,1024]{1,0:T(8,128)(2,1)}, u32[]{:S(2)}) copy-start(bf16[512,1024]{1,0:T(8,128)(2,1)} %param.18) | copy-start | bytes 3145732
  45.9 6.0 %copy-start.5 = (bf16[512,1024]{1,0:T(8,128)(2,1)S(1)}, bf16[512,1024]{1,0:T(8,128)(2,1)}, u32[]{:S(2)}) copy-start(bf16[512,1024]{1,0:T(8,128)(2,1)} %param.17) | copy-start | bytes 3145732
  52.8 18.0 %all-to-all-start.2 = ((bf16[8,64,1024]{2,1,0:T(8,128)(2,1)}), bf16[8,64,1024]{2,1,0:T(8,128)(2,1)S(1)}, u32[]{:S(2)}, u32[]{:S(2)}) async-start(bf16[8,64,1024]{2,1,0:T(8,128)(2,1)} %copy.55), calls=%async_computation.2 | async-start | bytes 2097152 | tf_op jit(solution)/shard_map/all_to_all | solution.py:89
  57.9 62.1 %copy-start.3 = (bf16[3,384]{1,0:T(4,128)(2,1)S(1)}, bf16[3,384]{1,0:T(4,128)(2,1)}, u32[]{:S(2)}) copy-start(bf16[3,384]{1,0:T(4,128)(2,1)} %param.22) | copy-start | bytes 6916
  70.8 17.9 %all-to-all-start.1 = ((bf16[8,64,1024]{2,1,0:T(8,128)(2,1)}), bf16[8,64,1024]{2,1,0:T(8,128)(2,1)S(1)}, u32[]{:S(2)}, u32[]{:S(2)}) async-start(bf16[8,64,1024]{2,1,0:T(8,128)(2,1)} %copy.53), calls=%async_computation.1 | async-start | bytes 2097152 | tf_op jit(solution)/shard_map/all_to_all | solution.py:88
  74.3 223.3 %reduce-scatter.2.cloned.1.call-start = ((), (), s32[]{:S(2)}) async-start(), calls=%async_computation.6 | async-start | bytes 2654208 | tf_op jit(solution)/shard_map/reduce_scatter | solution.py:136
Sparse Core Ops, SparseCore 0:
  9.5 56.6 all-gather.2
  68.2 51.7 all-gather.4
  229.9 67.6 reduce-scatter.1
where the time goes:
time: 308 us; the launch traced here: 306 us
  waiting for transfers between devices  125 us (41%)
  matrix products  66 us (21%)
  loops' own time  35.5 us (12%)
  local copies, waits for them, and re-layouts  33.6 us (11%)
  starting transfers between devices  19.6 us (6%)
  between operations  13.3 us (4%)
  other arithmetic  13.1 us (4%)
    reduce_scatter x1, waiting for transfers between devices, body(): lax.psum_scatter((lax.fori_loop(0, slot_count, add_slot, start_acc) * inv...  67.9 us
    all_gather x1, waiting for transfers between devices, body(): lax.all_gather(w_up, 'seq', axis=2, tiled=True)  31.4 us
    dot_general x8, matrix products, add_slot(): lax.dot_general(columns, grad_all[slot_idx], (((0,), (0,)), ((), ())), pr...  23.6 us
    another operation x1, loops' own time, body(): lax.map(slot_terms, (got_rows, got_cot, safe_lang, live_slot))  22.4 us
    dynamic_slice x16, local copies, waits for them, and re-layouts, body(): lax.map(slot_terms, (got_rows, got_cot, safe_lang, live_slot))  16.1 us
    another operation x1, loops' own time, body(): lax.fori_loop(0, slot_count, add_slot, start_acc) * inv_scale  13.2 us
    all_to_all x1, waiting for transfers between devices, body(): lax.all_to_all(row_slots, 'grp', split_axis=0, concat_axis=0, tiled=True)  12.8 us
    dot_general x8, matrix products, slot_terms(): lax.dot_general(slot_cot, up_one, (((1,), (1,)), ((), ())), preferred_ele...  12.1 us
  transfers between devices with their start and end apart: 8, of which 4 were waited for; matrix products, arithmetic and copies ran while one was open for 12% of the time, Pallas kernels for 0%

commit v1 on v0

--- a/solution.py
+++ b/solution.py
@@ -91,7 +91,7 @@
     )
     down_all, up_all = (
         lax.all_gather(w_down, "seq", axis=1, tiled=True),
-        lax.all_gather(w_up, "seq", axis=2, tiled=True),
+        jnp.concatenate(lax.all_gather(w_up, "seq"), axis=2),
     )
     live_slot = got_lang >= 0
     safe_lang = jnp.where(live_slot, got_lang - lax.axis_index("grp") * lang_grp, 0).astype(

time: 308 us -> 296 us (0.961)
  loops' own time: 35.5 us -> 31.3 us
  waiting for transfers between devices: 125 us -> 121 us
  local copies, waits for them, and re-layouts: 33.6 us -> 30.1 us
    all_gather x1, waiting for transfers between devices: 31.4 us -> 0.01 us  [body(): lax.all_gather(w_up, 'seq')]
    all_gather x1, waiting for transfers between devices: 0.01 us -> 30.1 us  [body(): lax.all_gather(w_down, 'seq', axis=1, tiled=True)]
    dynamic_slice x16, local copies, waits for them, and re-layouts: 16.1 us -> 9.3 us  [body(): lax.map(slot_terms, (got_rows, got_cot, safe_lang, live_slot))]
    another operation x1, loops' own time: 22.4 us -> 18.2 us  [body(): lax.map(slot_terms, (got_rows, got_cot, safe_lang, live_slot))]
    reshape x0 -> x1, local copies, waits for them, and re-layouts: none -> 3.85 us  [body(): jnp.concatenate(lax.all_gather(w_up, 'seq'), axis=2)]
  transfers between devices with their start and end apart: 8 -> 8, of which waited for: 4 -> 4; matrix products, arithmetic and copies ran while one was open for 12% -> 13% of each run, Pallas kernels for 0% -> 0%
where the time goes in v1:
time: 296 us; the launch traced here: 294 us
  waiting for transfers between devices  121 us (41%)
  matrix products  66 us (22%)
  loops' own time  31.3 us (11%)
  local copies, waits for them, and re-layouts  30.1 us (10%)
  starting transfers between devices  19.6 us (7%)
  between operations  13.3 us (4%)
  other arithmetic  12.5 us (4%)
    reduce_scatter x1, waiting for transfers between devices, body(): lax.psum_scatter((lax.fori_loop(0, slot_count, add_slot, start_acc) * inv...  68.3 us
    all_gather x1, waiting for transfers between devices, body(): lax.all_gather(w_down, 'seq', axis=1, tiled=True)  30.1 us
    dot_general x8, matrix products, add_slot(): lax.dot_general(columns, grad_all[slot_idx], (((0,), (0,)), ((), ())), pr...  23.6 us
    another operation x1, loops' own time, body(): lax.map(slot_terms, (got_rows, got_cot, safe_lang, live_slot))  18.2 us
    another operation x1, loops' own time, body(): lax.fori_loop(0, slot_count, add_slot, start_acc) * inv_scale  13.2 us
    dot_general x8, matrix products, slot_terms(): lax.dot_general(slot_cot, up_one, (((1,), (1,)), ((), ())), preferred_ele...  12.1 us
    all_to_all x1, waiting for transfers between devices, body(): lax.all_to_all(cot_slots, 'grp', split_axis=0, concat_axis=0, tiled=True)  11.3 us
    dot_general x8, matrix products, slot_terms(): jnp.dot(slot_rows, down_one, preferred_element_type=jnp.float32) + bias_one  11.1 us
  transfers between devices with their start and end apart: 8, of which 4 were waited for; matrix products, arithmetic and copies ran while one was open for 13% of the time, Pallas kernels for 0%

profile of v1, /device:TPU:0, one launch (start us, length us, event | category | flops | bytes accessed | tf_op | source)
XLA Modules:
  0.0 294.1 jit_solution(3364677107052313102)
XLA Ops:
  8.2 5.6 %collective-permute-start.1 = (bf16[256,512]{1,0:T(8,128)(2,1)S(1)}, bf16[256,512]{1,0:T(8,128)(2,1)}, u32[]{:S(2)}, u32[]{:S(2)}) collective-permute-start(bf16[256,512]{1,0:T(8,128)(2,1)S(1)} %slice.7), channel_id=1, source_target_pairs={{0,1},{1,2},{2,3},{3,4},{4,5},{5,6},{6,7},{8,9},{9,10},{10,11},{11... | collective-permute-start | bytes 786440 | tf_op jit(solution)/shard_map/ppermute | solution.py:15
  13.8 1.7 slice.6
  15.5 3.5 %collective-permute-start = (bf16[256,512]{1,0:T(8,128)(2,1)}, bf16[256,512]{1,0:T(8,128)(2,1)}, u32[]{:S(2)}, u32[]{:S(2)}) collective-permute-start(bf16[256,512]{1,0:T(8,128)(2,1)} %slice.6), channel_id=1, source_target_pairs={{0,1},{1,2},{2,3},{3,4},{4,5},{5,6},{6,7},{8,9},{9,10},{10,11},{11... | collective-permute-start | bytes 786440 | tf_op jit(solution)/shard_map/ppermute | solution.py:15
  22.0 3.2 %all-to-all-start = ((s32[4,2,1]{1,2,0:T(1,128)}), s32[4,2,1]{1,2,0:T(1,128)S(1)}, u32[]{:S(2)}, u32[]{:S(2)}) async-start(s32[4,2,1]{1,2,0:T(1,128)} %bitcast.11), calls=%async_computation | async-start | bytes 4096 | tf_op jit(solution)/shard_map/all_to_all | solution.py:90
  25.9 2.1 copy.54
  28.7 1.6 copy.59
  30.3 1.1 fusion.39
  31.4 1.0 pad_maximum_fusion.1
  32.4 1.2 copy.53
  33.6 11.0 %fusion.53 = (f32[8,512]{1,0:T(8,128)S(1)}, f32[8,512,768]{1,2,0:T(8,128)}) fusion(f32[512,768]{0,1:T(8,128)S(1)} %get-tuple-element.273, bf16[768,8,64]{0,2,1:T(8,128)(2,1)} %bitcast.93, bf16[512,8,64]{0,2,1:T(8,128)(2,1)} %bitcast.95, pred[512,768]{0,1:T(8,128)(4,1)} %get-tuple-element.272), kind=kOutput, calls=%fused_computation.86 | convolution fusion | flops 418382592 | bytes 15876096 | tf_op jit(solution)/shard_map/sub | solution.py:52
  45.9 6.0 %fusion.40 = bf16[8,64,512]{2,1,0:T(8,128)(2,1)S(1)} fusion(bf16[768,8,64]{0,2,1:T(8,128)(2,1)S(1)} %bitcast.94, f32[8,512,768]{1,2,0:T(8,128)} %get-tuple-element.275, f32[8,512]{1,0:T(8,128)S(1)} %get-tuple-element.274), kind=kOutput, calls=%fused_computation.57 | convolution fusion | flops 409206784 | bytes 13910016 | tf_op jit(solution)/shard_map/hqk,khd->qhd/dot_general | solution.py:54
  52.8 3.7 %all-to-all-start.2 = ((bf16[8,64,1024]{2,1,0:T(8,128)(2,1)}), bf16[8,64,1024]{2,1,0:T(8,128)(2,1)S(1)}, u32[]{:S(2)}, u32[]{:S(2)}) async-start(bf16[8,64,1024]{2,1,0:T(8,128)(2,1)} %copy.59), calls=%async_computation.2 | async-start | bytes 2097152 | tf_op jit(solution)/shard_map/all_to_all | solution.py:89
  57.9 1.6 copy.57
  59.5 11.3 %all-to-all-done.2 = bf16[8,64,1024]{2,1,0:T(8,128)(2,1)S(1)} async-done(((bf16[8,64,1024]{2,1,0:T(8,128)(2,1)}), bf16[8,64,1024]{2,1,0:T(8,128)(2,1)S(1)}, u32[]{:S(2)}, u32[]{:S(2)}) %all-to-all-start.2) | async-done | bytes 1048608 | tf_op jit(solution)/shard_map/all_to_all | solution.py:89
  70.8 3.5 %all-to-all-start.1 = ((bf16[8,64,1024]{2,1,0:T(8,128)(2,1)}), bf16[8,64,1024]{2,1,0:T(8,128)(2,1)S(1)}, u32[]{:S(2)}, u32[]{:S(2)}) async-start(bf16[8,64,1024]{2,1,0:T(8,128)(2,1)} %copy.57), calls=%async_computation.1 | async-start | bytes 2097152 | tf_op jit(solution)/shard_map/all_to_all | solution.py:88
  74.6 3.8 %copy.68 = bf16[8,3,48,8,128]{4,3,0,2,1:T(8,128)(2,1)} copy(bf16[8,3,48,8,128]{4,3,2,1,0:T(8,128)(2,1)} %bitcast.91) | data formatting | bytes 4718592 | tf_op jit(solution)/shard_map/reshape | solution.py:94
  78.5 10.2 %all-to-all-done.1 = bf16[8,64,1024]{2,1,0:T(8,128)(2,1)S(1)} async-done(((bf16[8,64,1024]{2,1,0:T(8,128)(2,1)}), bf16[8,64,1024]{2,1,0:T(8,128)(2,1)S(1)}, u32[]{:S(2)}, u32[]{:S(2)}) %all-to-all-start.1) | async-done | bytes 1048608 | tf_op jit(solution)/shard_map/all_to_all | solution.py:88
  88.7 30.1 %all-gather.4.cloned.1.call-done = bf16[3,1024,384]{2,1,0:T(8,128)(2,1)} async-done(((bf16[3,128,384]{2,1,0:T(8,128)(2,1)}), bf16[3,1024,384]{2,1,0:T(8,128)(2,1)}) %all-gather.4.cloned.1.call-update) | async-done | bytes 2359312 | tf_op jit(solution)/shard_map/all_gather | solution.py:93
  118.8 50.8 %while.25 = (s32[]{:T(128)}, bf16[8,64,384]{2,1,0:T(8,128)(2,1)S(1)}, bf16[8,64,1024]{2,1,0:T(8,128)(2,1)S(1)}, s32[8]{0:T(128)S(1)}, bf16[3,1024,384]{2,1,0:T(8...) while((s32[]{:T(128)}, ...), condition=%wide.region_8.9_spmd, body=%wide.region_7.8_spmd.sunk | while | flops 101179776 | bytes 2087354 | solution.py:117
  121.1 1.4 convolution_add_fusion.2
  123.6 1.5 fusion.73
  127.4 1.4 convolution_add_fusion.2
  130.0 1.5 fusion.73
  133.8 1.4 convolution_add_fusion.2
  136.3 1.5 fusion.73
  140.1 1.4 convolution_add_fusion.2
  142.7 1.5 fusion.73
  146.5 1.4 convolution_add_fusion.2
  149.0 1.5 fusion.73
  152.8 1.4 convolution_add_fusion.2
  155.4 1.5 fusion.73
  159.2 1.4 convolution_add_fusion.2
  161.7 1.5 fusion.73
  165.5 1.4 convolution_add_fusion.2
  168.1 1.5 fusion.73
  169.6 2.4 broadcast_in_dim.50
  172.0 41.2 %while.26 = (s32[]{:T(128)}, f32[1024,3,384]{2,0,1:T(8,128)}, s32[8]{0:T(128)S(1)}, bf16[8,64,1024]{2,1,0:T(8,128)(2,1)S(1)}, bf16[8,64,384]{2,1,0:T(8,128)(2,1)S(1)}, /*index=5*/s32[]{:T(128)}, s32[]{:T(128)}, s32[]{:T(128)}) while((s32[]{:T(128)}, f32[1024,3,384]{2,0,1:T(8,128)}, s32[8]{0:T(128)S(1)}, bf16[8,64,1024]{2,1,0:T(8,128)(2,1)S(1)}, ...), condition=%wide.region_10.11_spmd, body=%wide.region_9.10_spmd.sunk | while | flops 50724868 | bytes 3327111 | solution.py:137
  174.2 3.0 %fusion.76 = f32[1024,3,384]{2,0,1:T(8,128)} fusion(f32[1024,3,384]{2,0,1:T(8,128)} %get-tuple-element.409, s32[]{:T(128)S(6)} %select_n.61, bf16[8,64,1024]{2,1,0:T(8,128)(2,1)S(1)} %get-tuple-element.419, s32[]{:T(128)} %get-tuple-element.408, bf16[8,64,384]{2,1,0:T(8,128)(2,1)S(1)} %get-tuple-element.420), kind=kOutput, calls=%fused_computation.1.clone.1 | convolution fusion | flops 50724864 | bytes 3326980 | tf_op jit(solution)/shard_map/while/body/eval_jaxpr/dot_general | solution.py:122
  179.4 3.0 %fusion.76 = f32[1024,3,384]{2,0,1:T(8,128)} fusion(f32[1024,3,384]{2,0,1:T(8,128)} %get-tuple-element.409, s32[]{:T(128)S(6)} %select_n.61, bf16[8,64,1024]{2,1,0:T(8,128)(2,1)S(1)} %get-tuple-element.419, s32[]{:T(128)} %get-tuple-element.408, bf16[8,64,384]{2,1,0:T(8,128)(2,1)S(1)} %get-tuple-element.420), kind=kOutput, calls=%fused_computation.1.clone.1 | convolution fusion | flops 50724864 | bytes 3326980 | tf_op jit(solution)/shard_map/while/body/eval_jaxpr/dot_general | solution.py:122
  184.5 2.9 %fusion.76 = f32[1024,3,384]{2,0,1:T(8,128)} fusion(f32[1024,3,384]{2,0,1:T(8,128)} %get-tuple-element.409, s32[]{:T(128)S(6)} %select_n.61, bf16[8,64,1024]{2,1,0:T(8,128)(2,1)S(1)} %get-tuple-element.419, s32[]{:T(128)} %get-tuple-element.408, bf16[8,64,384]{2,1,0:T(8,128)(2,1)S(1)} %get-tuple-element.420), kind=kOutput, calls=%fused_computation.1.clone.1 | convolution fusion | flops 50724864 | bytes 3326980 | tf_op jit(solution)/shard_map/while/body/eval_jaxpr/dot_general | solution.py:122
  189.7 2.9 %fusion.76 = f32[1024,3,384]{2,0,1:T(8,128)} fusion(f32[1024,3,384]{2,0,1:T(8,128)} %get-tuple-element.409, s32[]{:T(128)S(6)} %select_n.61, bf16[8,64,1024]{2,1,0:T(8,128)(2,1)S(1)} %get-tuple-element.419, s32[]{:T(128)} %get-tuple-element.408, bf16[8,64,384]{2,1,0:T(8,128)(2,1)S(1)} %get-tuple-element.420), kind=kOutput, calls=%fused_computation.1.clone.1 | convolution fusion | flops 50724864 | bytes 3326980 | tf_op jit(solution)/shard_map/while/body/eval_jaxpr/dot_general | solution.py:122
  194.8 2.9 %fusion.76 = f32[1024,3,384]{2,0,1:T(8,128)} fusion(f32[1024,3,384]{2,0,1:T(8,128)} %get-tuple-element.409, s32[]{:T(128)S(6)} %select_n.61, bf16[8,64,1024]{2,1,0:T(8,128)(2,1)S(1)} %get-tuple-element.419, s32[]{:T(128)} %get-tuple-element.408, bf16[8,64,384]{2,1,0:T(8,128)(2,1)S(1)} %get-tuple-element.420), kind=kOutput, calls=%fused_computation.1.clone.1 | convolution fusion | flops 50724864 | bytes 3326980 | tf_op jit(solution)/shard_map/while/body/eval_jaxpr/dot_general | solution.py:122
  200.0 2.9 %fusion.76 = f32[1024,3,384]{2,0,1:T(8,128)} fusion(f32[1024,3,384]{2,0,1:T(8,128)} %get-tuple-element.409, s32[]{:T(128)S(6)} %select_n.61, bf16[8,64,1024]{2,1,0:T(8,128)(2,1)S(1)} %get-tuple-element.419, s32[]{:T(128)} %get-tuple-element.408, bf16[8,64,384]{2,1,0:T(8,128)(2,1)S(1)} %get-tuple-element.420), kind=kOutput, calls=%fused_computation.1.clone.1 | convolution fusion | flops 50724864 | bytes 3326980 | tf_op jit(solution)/shard_map/while/body/eval_jaxpr/dot_general | solution.py:122
  205.1 3.0 %fusion.76 = f32[1024,3,384]{2,0,1:T(8,128)} fusion(f32[1024,3,384]{2,0,1:T(8,128)} %get-tuple-element.409, s32[]{:T(128)S(6)} %select_n.61, bf16[8,64,1024]{2,1,0:T(8,128)(2,1)S(1)} %get-tuple-element.419, s32[]{:T(128)} %get-tuple-element.408, bf16[8,64,384]{2,1,0:T(8,128)(2,1)S(1)} %get-tuple-element.420), kind=kOutput, calls=%fused_computation.1.clone.1 | convolution fusion | flops 50724864 | bytes 3326980 | tf_op jit(solution)/shard_map/while/body/eval_jaxpr/dot_general | solution.py:122
  210.3 2.9 %fusion.76 = f32[1024,3,384]{2,0,1:T(8,128)} fusion(f32[1024,3,384]{2,0,1:T(8,128)} %get-tuple-element.409, s32[]{:T(128)S(6)} %select_n.61, bf16[8,64,1024]{2,1,0:T(8,128)(2,1)S(1)} %get-tuple-element.419, s32[]{:T(128)} %get-tuple-element.408, bf16[8,64,384]{2,1,0:T(8,128)(2,1)S(1)} %get-tuple-element.420), kind=kOutput, calls=%fused_computation.1.clone.1 | convolution fusion | flops 50724864 | bytes 3326980 | tf_op jit(solution)/shard_map/while/body/eval_jaxpr/dot_general | solution.py:122
  213.2 4.2 %multiply_convert_fusion = bf16[1024,3,384]{2,0,1:T(8,128)(2,1)} fusion(f32[1024,3,384]{2,0,1:T(8,128)} %get-tuple-element.213), kind=kLoop, calls=%fused_computation.42 | loop fusion | flops 2359296 | bytes 7077888 | tf_op jit(solution)/shard_map/convert_element_type | solution.py:137
  217.4 68.3 %reduce-scatter.2.cloned.1.call-done = bf16[128,3,384]{2,0,1:T(8,128)(2,1)} async-done(((bf16[1024,3,384]{2,0,1:T(8,128)(2,1)}), bf16[128,3,384]{2,0,1:T(8,128)(2,1)}) %reduce-scatter.2.cloned.1.call-update) | async-done | bytes 294928 | tf_op jit(solution)/shard_map/reduce_scatter | solution.py:136
  285.7 1.8 convert_element_type.84
  (78 shorter events, 23.9 us)
Async XLA Ops:
  6.5 21.5 %copy-start = (bf16[512,1024]{1,0:T(8,128)(2,1)S(1)}, bf16[512,1024]{1,0:T(8,128)(2,1)}, u32[]{:S(2)}) copy-start(bf16[512,1024]{1,0:T(8,128)(2,1)} %param.23) | copy-start | bytes 3145732
  6.5 68.1 %all-gather.6.cloned.1.call-start = ((), (), s32[]{:S(2)}) async-start(), calls=%async_computation.6 | async-start | bytes 2654208 | tf_op jit(solution)/shard_map/all_gather | solution.py:94
  8.2 23.2 %collective-permute-start.1 = (bf16[256,512]{1,0:T(8,128)(2,1)S(1)}, bf16[256,512]{1,0:T(8,128)(2,1)}, u32[]{:S(2)}, u32[]{:S(2)}) collective-permute-start(bf16[256,512]{1,0:T(8,128)(2,1)S(1)} %slice.7), channel_id=1, source_target_pairs={{0,1},{1,2},{2,3},{3,4},{4,5},{5,6},{6,7},{8,9},{9,10},{10,11},{11... | collective-permute-start | bytes 786440 | tf_op jit(solution)/shard_map/ppermute | solution.py:15
  15.5 29.1 %collective-permute-start = (bf16[256,512]{1,0:T(8,128)(2,1)}, bf16[256,512]{1,0:T(8,128)(2,1)}, u32[]{:S(2)}, u32[]{:S(2)}) collective-permute-start(bf16[256,512]{1,0:T(8,128)(2,1)} %slice.6), channel_id=1, source_target_pairs={{0,1},{1,2},{2,3},{3,4},{4,5},{5,6},{6,7},{8,9},{9,10},{10,11},{11... | collective-permute-start | bytes 786440 | tf_op jit(solution)/shard_map/ppermute | solution.py:15
  22.0 30.8 %all-to-all-start = ((s32[4,2,1]{1,2,0:T(1,128)}), s32[4,2,1]{1,2,0:T(1,128)S(1)}, u32[]{:S(2)}, u32[]{:S(2)}) async-start(s32[4,2,1]{1,2,0:T(1,128)} %bitcast.11), calls=%async_computation | async-start | bytes 4096 | tf_op jit(solution)/shard_map/all_to_all | solution.py:90
  25.2 93.6 %all-gather.4.cloned.1.call-start = ((), (), s32[]{:S(2)}) async-start(), calls=%async_computation.4 | async-start | bytes 2654208 | tf_op jit(solution)/shard_map/all_gather | solution.py:93
  28.7 2.7 copy-start.1
  33.6 11.0 %copy-start.2 = (bf16[512,512]{1,0:T(8,128)(2,1)S(1)}, bf16[512,512]{1,0:T(8,128)(2,1)}, u32[]{:S(2)}) copy-start(bf16[512,512]{1,0:T(8,128)(2,1)} %param.16) | copy-start | bytes 1572868
  45.9 6.0 %copy-start.4 = (bf16[512,1024]{1,0:T(8,128)(2,1)S(1)}, bf16[512,1024]{1,0:T(8,128)(2,1)}, u32[]{:S(2)}) copy-start(bf16[512,1024]{1,0:T(8,128)(2,1)} %param.18) | copy-start | bytes 3145732
  45.9 6.0 %copy-start.5 = (bf16[512,1024]{1,0:T(8,128)(2,1)S(1)}, bf16[512,1024]{1,0:T(8,128)(2,1)}, u32[]{:S(2)}) copy-start(bf16[512,1024]{1,0:T(8,128)(2,1)} %param.17) | copy-start | bytes 3145732
  52.8 18.0 %all-to-all-start.2 = ((bf16[8,64,1024]{2,1,0:T(8,128)(2,1)}), bf16[8,64,1024]{2,1,0:T(8,128)(2,1)S(1)}, u32[]{:S(2)}, u32[]{:S(2)}) async-start(bf16[8,64,1024]{2,1,0:T(8,128)(2,1)} %copy.59), calls=%async_computation.2 | async-start | bytes 2097152 | tf_op jit(solution)/shard_map/all_to_all | solution.py:89
  70.8 17.9 %all-to-all-start.1 = ((bf16[8,64,1024]{2,1,0:T(8,128)(2,1)}), bf16[8,64,1024]{2,1,0:T(8,128)(2,1)S(1)}, u32[]{:S(2)}, u32[]{:S(2)}) async-start(bf16[8,64,1024]{2,1,0:T(8,128)(2,1)} %copy.57), calls=%async_computation.1 | async-start | bytes 2097152 | tf_op jit(solution)/shard_map/all_to_all | solution.py:88
  74.3 211.4 %reduce-scatter.2.cloned.1.call-start = ((), (), s32[]{:S(2)}) async-start(), calls=%async_computation.5 | async-start | bytes 2654208 | tf_op jit(solution)/shard_map/reduce_scatter | solution.py:136
  74.6 44.1 %copy-start.3 = (bf16[3,384]{1,0:T(4,128)(2,1)S(1)}, bf16[3,384]{1,0:T(4,128)(2,1)}, u32[]{:S(2)}) copy-start(bf16[3,384]{1,0:T(4,128)(2,1)} %param.22) | copy-start | bytes 6916
Sparse Core Ops, SparseCore 0:
  9.5 56.6 all-gather.5
  68.4 50.3 all-gather.3
  217.6 68.1 reduce-scatter.1
